TPU v7x, 32 devices: a whole 2x2x4 slice. The times are simulated.
32 devices in a mesh: tile: 8 (over y, x, core), body: 4 (over z).
Axes of the slice: x: 2, y: 2, z: 4, core: 2. Of those that a mesh axis runs over, the one named last changes fastest.
Arguments:
- fluid_position: float32 [3, 128, 32, 128], P(None, 'tile', 'body'), may hold values from 0 to 128, as said below
- fluid_pressure: float32 [128, 32, 128], P('tile', 'body'), may hold values from 0 to 1
- source: float32 [128, 32, 128], P('tile', 'body'), may hold values from -12 to 12
- stiffness: float32 [128, 32, 128], P('tile', 'body'), may hold values from 0.5 to 2
- neighbours: int32 [128, 32, 6], P('tile', 'body'), may hold values from 0 to 8, as said below
- wall_position: float32 [3, 128, 32, 128], P(None, 'tile', 'body'), may hold values from 0 to 128, as said below
- wall_normal: float32 [3, 128, 32, 128], P(None, 'tile', 'body'), may hold values from -4 to 4
- wall_arm: float32 [3, 128, 32, 128], P(None, 'tile', 'body'), may hold values from -4 to 4
- wall_live: int32 [128, 32, 128], P('tile', 'body'), may hold values 0 or 1
- wall_body: int32 [128, 32, 128], P('tile', 'body'), may hold values from 0 to 30719, as said below
- linear_velocity: float32 [3, 30720], P(None, 'body'), may hold values from -6 to 6
- angular_velocity: float32 [3, 30720], P(None, 'body'), may hold values from -6 to 6
- inverse_mass: float32 [30720], P('body'), may hold values from 0.2 to 2
- inverse_inertia: float32 [3, 30720], P(None, 'body'), may hold values from 0.2 to 2
Outputs:
- pressure: float32 [128, 32, 128], P('tile', 'body')
- wall_pressure: float32 [128, 32, 128], P('tile', 'body')
- body_state: float32 [6, 30720], P(None, 'body')
- wall_velocity: float32 [3, 128, 32, 128], P(None, 'tile', 'body')
- density_error: float32 [], replicated
Inputs may be any that keep to these rules, and one draw needn't show every extreme that they name: `neighbours`: entry 0 of every list is 4, the block itself; the other entries are distinct codes of the eight blocks around it. `fluid_position`: A particle of block (a, b) has its first coordinate in [a, a + 1), its second in [b, b + 1), its third in [0, 1). `wall_position`: A particle of block (a, b) has its first coordinate in [a, a + 1], its second in [b, b + 1], its third in [0, 1]. `wall_body`: bodies are compact: a boundary particle belongs to a body whose centre lies within a few blocks of its own block.
All inputs are finite; a program needn't handle non-finite values. No bound on the sum of `wall_live` on one device may be relied on, other than what follows from the above.
Results may differ from a plain program's by a relative error of at most 0.0003.
Values sent between devices are 32-bit elements; how exact they have to be, the bound alone decides.
A program may use at most 128 MiB of HBM per device.

v0:
```python
import jax
import jax.numpy as jnp
from jax import lax
from jax.sharding import PartitionSpec as P

SWEEPS = 2
BODIES = 30720
relax_factor = 0.5
inv_width = 2.0
kernel_scale = 0.0078125
wall_offset = 0.5
time_step = 0.25
gravity_z = -9.81


def padded(block, sides, width):
    for axis, dim in sides:
        count = lax.axis_size(axis)
        forward = [(i, i + 1) for i in range(count - 1)]
        backward = [(target, source) for source, target in forward]
        low = lax.ppermute(
            lax.slice_in_dim(block, block.shape[dim] - width, None, axis=dim), axis, forward
        )
        high = lax.ppermute(lax.slice_in_dim(block, 0, width, axis=dim), axis, backward)
        block = jnp.concatenate([low, block, high], axis=dim)
    return block


def pair_sums(padded_pos, padded_val, own_pos, neighbours):
    row_count = own_pos.shape[1]
    columns = own_pos.shape[2]

    def one_row(row_index):
        window_pos = lax.dynamic_slice_in_dim(padded_pos, row_index, 3, 1)
        window_val = lax.dynamic_slice_in_dim(padded_val, row_index, 3, 0)
        shifted_pos = jnp.stack(
            [window_pos[:, i, j : j + columns] for i in range(3) for j in range(3)], 0
        )
        shifted_val = jnp.stack(
            [window_val[i, j : j + columns] for i in range(3) for j in range(3)], 0
        )
        code_list = lax.dynamic_index_in_dim(neighbours, row_index, 0, keepdims=False)
        near_pos = jnp.take_along_axis(
            jnp.transpose(shifted_pos, (2, 0, 1, 3)), code_list[:, :, None, None], axis=1
        )
        near_val = jnp.take_along_axis(
            jnp.transpose(shifted_val, (1, 0, 2)), code_list[:, :, None], axis=1
        )
        own_rows = lax.dynamic_index_in_dim(own_pos, row_index, 1, keepdims=False)
        distance = None
        for component in range(3):
            offset = (
                own_rows[component][:, None, :, None] - near_pos[:, :, component][:, :, None, :]
            )
            distance = offset * offset if distance is None else distance + offset * offset
        weight = jnp.exp(-distance * inv_width) * kernel_scale
        weight_sum = jnp.sum(weight, axis=(1, 3))
        weighted = jnp.einsum("ckij,ckj->ci", weight, near_val, precision=lax.Precision.HIGHEST)
        return (weight_sum, weighted)

    return lax.map(one_row, jnp.arange(row_count, dtype=jnp.int32))


def cross_product(left, right):
    return jnp.stack(
        [
            left[1] * right[2] - left[2] * right[1],
            left[2] * right[0] - left[0] * right[2],
            left[0] * right[1] - left[1] * right[0],
        ],
        0,
    )


def advance(params, totals):
    lift = jnp.array([0.0, 0.0, time_step * gravity_z], dtype=jnp.float32)[:, None]
    linear = params[0:3] + time_step * (params[6][None] * totals[0:3]) + lift
    angular = params[3:6] + time_step * params[7:10] * totals[3:6]
    return jnp.concatenate([linear, angular], 0)


def widened(values):
    return padded(values, (("tile", 0), ("body", 1)), 1)


def shards(
    fluid_position,
    fluid_pressure,
    source,
    stiffness,
    neighbours,
    wall_position,
    wall_normal,
    wall_arm,
    wall_live,
    wall_body,
    linear_velocity,
    angular_velocity,
    inverse_mass,
    inverse_inertia,
):
    padded_pos = padded(fluid_position, (("tile", 1), ("body", 2)), 1)
    pressure = fluid_pressure
    residual = source
    for sweep_index in range(SWEEPS):
        weight_sum, weighted = pair_sums(padded_pos, widened(pressure), fluid_position, neighbours)
        diagonal = stiffness + weight_sum
        residual = source - (diagonal * pressure - weighted)
        pressure = jnp.maximum(pressure + relax_factor * residual / diagonal, 0.0)
    particle_total = residual.size * lax.axis_size("tile") * lax.axis_size("body")
    error_local = jnp.sum(residual * residual) / particle_total
    weight_sum, weighted = pair_sums(padded_pos, widened(pressure), wall_position, neighbours)
    wall_pressure = weighted / (wall_offset + weight_sum) * wall_live.astype(jnp.float32)
    force = wall_pressure[None] * wall_normal
    torque = cross_product(wall_arm, force)
    stacked = jnp.concatenate([force, torque], 0).reshape(6, -1).T
    partials = jax.ops.segment_sum(stacked, wall_body.reshape(-1), num_segments=BODIES).T
    owned = BODIES // lax.axis_size("body")
    first_owned = lax.axis_index("body") * owned
    own_params = jnp.concatenate(
        [linear_velocity, angular_velocity, inverse_mass[None], inverse_inertia], 0
    )
    totals, density_error = lax.psum((partials, error_local), ("tile", "body"))
    all_params = lax.all_gather(own_params, "body", axis=1, tiled=True)
    full_state = advance(all_params, totals)
    own_state = lax.dynamic_slice_in_dim(full_state, first_owned, owned, 1)
    index_flat = wall_body.reshape(-1)
    moving = jnp.take(full_state[0:3], index_flat, axis=1).reshape(wall_arm.shape)
    turning = jnp.take(full_state[3:6], index_flat, axis=1).reshape(wall_arm.shape)
    wall_velocity = moving + cross_product(turning, wall_arm)
    return (pressure, wall_pressure, own_state, wall_velocity, density_error)


def solution(mesh):
    placed = (
        P(None, "tile", "body", None),
        P("tile", "body", None),
        P("tile", "body", None),
        P("tile", "body", None),
        P("tile", "body", None),
        P(None, "tile", "body", None),
        P(None, "tile", "body", None),
        P(None, "tile", "body", None),
        P("tile", "body", None),
        P("tile", "body", None),
        P(None, "body"),
        P(None, "body"),
        P("body"),
        P(None, "body"),
    )
    return jax.shard_map(
        shards,
        mesh=mesh,
        in_specs=placed,
        out_specs=(
            P("tile", "body", None),
            P("tile", "body", None),
            P(None, "body"),
            P(None, "tile", "body", None),
            P(),
        ),
        check_vma=False,
    )
```

profile of v0, /device:TPU:0, one launch (start us, length us, event | category | flops | bytes accessed | tf_op | source)
XLA Modules:
  0.0 1128.1 jit_solution(10268399384290714096)
XLA Ops:
  13.8 4.5 collective-permute-start
  27.3 4.5 collective-permute-start.2
  33.4 4.2 collective-permute-done.3
  37.9 214.2 %while.36 = (s32[]{:T(128)}, f32[16,8,128]{2,1,0:T(8,128)S(1)}, f32[16,8,128]{2,1,0:T(8,128)S(1)}, s32[16]{0:T(128)S(1)}, f32[3,16,8,128]{3,2,1,0:T(8,128)}, /*i...) while((s32[]{:T(128)}, f32[16,8,128]{2,1,0:T(8,128)S(1)}, ...), condition=%wide.region_2.0_spmd, body=%wide.region_0.4_spmd.sunk | while | flops 27549932 | bytes 1204188 | solution.py:61
  47.2 4.0 fusion.81
  60.6 4.0 fusion.81
  74.0 4.0 fusion.81
  87.4 4.0 fusion.81
  100.8 4.0 fusion.81
  114.1 4.0 fusion.81
  127.5 4.0 fusion.81
  140.9 4.0 fusion.81
  154.3 4.0 fusion.81
  167.7 4.0 fusion.81
  181.1 4.0 fusion.81
  194.5 4.0 fusion.81
  207.8 4.0 fusion.81
  221.2 4.0 fusion.81
  234.6 4.0 fusion.81
  248.0 4.0 fusion.81
  254.7 5.0 collective-permute-done.9
  264.7 4.0 collective-permute-done.11
  268.9 214.2 %while.37 = (s32[]{:T(128)}, f32[16,8,128]{2,1,0:T(8,128)S(1)}, f32[16,8,128]{2,1,0:T(8,128)S(1)}, s32[16]{0:T(128)S(1)}, f32[3,16,8,128]{3,2,1,0:T(8,128)}, /*i...) while((s32[]{:T(128)}, f32[16,8,128]{2,1,0:T(8,128)S(1)}, ...), condition=%wide.region_5.8_spmd, body=%wide.region_3.7_spmd.sunk | while | flops 27549932 | bytes 1204188 | solution.py:61
  278.2 4.0 fusion.85
  291.6 4.0 fusion.85
  305.0 4.0 fusion.85
  318.4 4.0 fusion.85
  331.8 4.0 fusion.85
  345.1 4.0 fusion.85
  358.5 4.0 fusion.85
  371.9 4.0 fusion.85
  385.3 4.0 fusion.85
  398.7 4.0 fusion.85
  412.1 4.0 fusion.85
  425.5 4.0 fusion.85
  438.8 4.0 fusion.85
  452.2 4.0 fusion.85
  465.6 4.0 fusion.85
  479.0 4.0 fusion.85
  500.0 214.1 %while.38 = (s32[]{:T(128)}, f32[16,8,128]{2,1,0:T(8,128)S(1)}, f32[16,8,128]{2,1,0:T(8,128)S(1)}, s32[16]{0:T(128)S(1)}, f32[3,16,8,128]{3,2,1,0:T(8,128)}, /*i...) while((s32[]{:T(128)}, f32[16,8,128]{2,1,0:T(8,128)S(1)}, ...), condition=%wide.region_8.11_spmd, body=%wide.region_6.10_spmd.sunk | while | flops 27549932 | bytes 1204188 | solution.py:61
  509.3 4.0 fusion.89
  522.7 4.0 fusion.89
  536.1 4.0 fusion.89
  549.5 4.0 fusion.89
  562.9 4.0 fusion.89
  576.2 4.0 fusion.89
  589.6 4.0 fusion.89
  603.0 4.0 fusion.89
  616.4 4.0 fusion.89
  629.8 4.0 fusion.89
  643.2 4.0 fusion.89
  669.9 4.0 fusion.89
  714.7 5.3 copy.268
  719.9 94.0 %scatter_custom_fusion = f32[30720,6]{1,0:T(8,128)} fusion(s32[16384]{0:T(1024)S(1)} %bitcast.478, f32[16384,6]{1,0:T(8,128)} %copy.268, f32[]{:T(128)} %constant.113.clone.1), kind=kCustom, calls=%fused_computation.226 | custom fusion | flops 98304 | bytes 737792 | tf_op jit(solution)/shard_map/scatter-add | solution.py:117
  814.0 9.5 copy.269
  824.2 41.4 %psum.15 = f32[]{:T(128)} all-reduce(f32[]{:T(128)S(6)} %div.15), channel_id=1, replica_groups=mesh['tile'=8,'body'=4] {'tile','body'}, use_global_device_ids=true, to_apply=%region_12.16 | all-reduce | flops 1 | bytes 8 | tf_op jit(solution)/shard_map/psum | solution.py:123
  866.9 86.6 %all-reduce.2.cloned.1.call-done = f32[6,30720]{1,0:T(8,128)} async-done(((f32[6,30720]{1,0:T(8,128)}), f32[6,30720]{1,0:T(8,128)}) %all-reduce.2.cloned.1.call-update) | async-done | bytes 737296 | tf_op jit(solution)/shard_map/psum | solution.py:123
  956.9 7.7 copy.271
  964.6 7.7 copy.270
  973.2 59.8 %gather_fusion.7 = f32[16384,3]{1,0:T(8,128)} fusion(f32[3,30720]{0,1:T(8,128)} %copy.271, s32[16384]{0:T(1024)S(1)} %fusion.58), kind=kCustom, calls=%fused_computation.7.clone | custom fusion | bytes 458752 | tf_op jit(solution)/shard_map/jit(_take)/gather | solution.py:129
  1033.0 59.9 %gather_fusion.6 = f32[16384,3]{1,0:T(8,128)} fusion(f32[3,30720]{0,1:T(8,128)} %copy.270, s32[16384]{0:T(1024)S(1)} %fusion.58), kind=kCustom, calls=%fused_computation.2.clone | custom fusion | bytes 458752 | tf_op jit(solution)/shard_map/jit(_take)/gather | solution.py:128
  1092.8 10.8 select_bitcast_fusion.3
  1103.6 11.0 slice_reduce_fusion.1
  1114.6 5.2 copy.272
  (1887 shorter events, 350.7 us)
Async XLA Ops:
  8.0 857.6 %all-gather.2.cloned.1.call-start = ((), (), s32[]{:S(2)}) async-start(), calls=%async_computation | async-start | bytes 2457600 | tf_op jit(solution)/shard_map/all_gather | solution.py:124
  8.8 12.5 %collective-permute-start.5 = (f32[1,8,128]{2,1,0:T(8,128)S(1)}, f32[1,8,128]{2,1,0:T(8,128)S(1)}, u32[]{:S(2)}, u32[]{:S(2)}) collective-permute-start(f32[1,8,128]{2,1,0:T(8,128)S(1)} %get-tuple-element.378), channel_id=1, source_target_pairs={{4,0},{8,4},{12,8},{16,12},{20,16},{24,20},{28,24},{5,1},{9,5},{13... | collective-permute-start | bytes 12296 | tf_op jit(solution)/shard_map/ppermute | solution.py:24
  10.0 10.4 collective-permute-start.4
  13.8 12.3 %collective-permute-start = (f32[3,1,8,128]{3,0,2,1:T(4,128)S(1)}, f32[3,1,8,128]{3,0,2,1:T(4,128)S(1)}, u32[]{:S(2)}, u32[]{:S(2)}) collective-permute-start(f32[3,1,8,128]{3,0,2,1:T(4,128)S(1)} %copy.294), channel_id=1, source_target_pairs={{0,4},{4,8},{8,12},{12,16},{16,20},{20,24},{24,28},{1,5},{5,9},{9,... | collective-permute-start | bytes 36872 | tf_op jit(solution)/shard_map/ppermute | solution.py:21
  18.3 8.9 collective-permute-start.1
  21.3 11.8 %collective-permute-start.6 = (f32[18,1,128]{2,1,0:T(1,128)S(1)}, f32[18,1,128]{2,1,0:T(1,128)S(1)}, u32[]{:S(2)}, u32[]{:S(2)}) collective-permute-start(f32[18,1,128]{2,1,0:T(1,128)S(1)} %get-tuple-element.372), channel_id=1, source_target_pairs={{0,1},{1,2},{2,3},{4,5},{5,6},{6,7},{8,9},{9,10},{10,11},{12,13},{... | collective-permute-start | bytes 27656 | tf_op jit(solution)/shard_map/ppermute | solution.py:21
  24.8 8.3 collective-permute-start.7
  27.3 6.2 collective-permute-start.2
  31.8 5.9 collective-permute-start.3
  37.8 214.2 %copy-start.4 = (f32[16,8,128]{2,1,0:T(8,128)S(1)}, f32[16,8,128]{2,1,0:T(8,128)}, u32[]{:S(2)}) copy-start(f32[16,8,128]{2,1,0:T(8,128)} %param.28) | copy-start | bytes 196612
  37.8 214.2 %copy-start.6 = (f32[16,8,128]{2,1,0:T(8,128)S(1)}, f32[16,8,128]{2,1,0:T(8,128)}, u32[]{:S(2)}) copy-start(f32[16,8,128]{2,1,0:T(8,128)} %param.29) | copy-start | bytes 196612
  37.8 214.2 %copy-start.7 = (f32[16,8,128]{2,1,0:T(8,128)S(1)}, f32[16,8,128]{2,1,0:T(8,128)}, u32[]{:S(2)}) copy-start(f32[16,8,128]{2,1,0:T(8,128)} %param.30) | copy-start | bytes 196612
  37.8 226.8 %copy-start.12 = (f32[7680]{0:T(1024)S(1)}, f32[7680]{0:T(1024)}, u32[]{:S(2)}) copy-start(f32[7680]{0:T(1024)} %param.39) | copy-start | bytes 92164
  252.1 2.6 collective-permute-start.8
  253.4 6.3 collective-permute-start.9
  259.7 5.0 collective-permute-start.10
  263.2 5.6 collective-permute-start.11
  268.8 219.0 %copy-start.8 = (f32[3,7680]{1,0:T(4,128)S(1)}, f32[3,7680]{1,0:T(4,128)}, u32[]{:S(2)}) copy-start(f32[3,7680]{1,0:T(4,128)} %param.40) | copy-start | bytes 276484
  268.8 219.0 %copy-start.9 = (f32[3,7680]{1,0:T(4,128)S(1)}, f32[3,7680]{1,0:T(4,128)}, u32[]{:S(2)}) copy-start(f32[3,7680]{1,0:T(4,128)} %param.38) | copy-start | bytes 276484
  268.8 219.0 %copy-start.10 = (f32[3,7680]{1,0:T(4,128)S(1)}, f32[3,7680]{1,0:T(4,128)}, u32[]{:S(2)}) copy-start(f32[3,7680]{1,0:T(4,128)} %param.37) | copy-start | bytes 276484
  268.9 227.0 %copy-start.5 = (s32[16,8,128]{2,1,0:T(8,128)S(1)}, s32[16,8,128]{2,1,0:T(8,128)}, u32[]{:S(2)}) copy-start(s32[16,8,128]{2,1,0:T(8,128)} %param.36) | copy-start | bytes 196612
  483.7 16.3 %copy-start.2 = (f32[16,8,128]{2,1,0:T(8,128)}, f32[16,8,128]{2,1,0:T(8,128)S(1)}, u32[]{:S(2)}) copy-start(f32[16,8,128]{2,1,0:T(8,128)S(1)} %get-tuple-element.360) | copy-start | bytes 196612
  483.7 5.2 collective-permute-start.12
  486.5 4.3 collective-permute-start.13
  488.8 464.7 %all-reduce.2.cloned.1.call-start = ((), (), s32[]{:S(2)}) async-start(), calls=%async_computation.1 | async-start | bytes 1966080 | tf_op jit(solution)/shard_map/psum | solution.py:123
  490.8 5.1 collective-permute-start.14
  494.3 5.6 collective-permute-start.15
  499.9 214.2 %copy-start.11 = (s32[16,8,128]{2,1,0:T(8,128)S(1)}, s32[16,8,128]{2,1,0:T(8,128)}, u32[]{:S(2)}) copy-start(s32[16,8,128]{2,1,0:T(8,128)} %param.35) | copy-start | bytes 196612
  499.9 214.2 %copy-start = (f32[3,16,8,128]{3,2,1,0:T(8,128)S(1)}, f32[3,16,8,128]{3,2,1,0:T(8,128)}, u32[]{:S(2)}) copy-start(f32[3,16,8,128]{3,2,1,0:T(8,128)} %param.33) | copy-start | bytes 589828
  499.9 214.3 %copy-start.1 = (f32[3,16,8,128]{3,2,1,0:T(8,128)S(1)}, f32[3,16,8,128]{3,2,1,0:T(8,128)}, u32[]{:S(2)}) copy-start(f32[3,16,8,128]{3,2,1,0:T(8,128)} %param.34) | copy-start | bytes 589828
  714.2 5.8 copy-start.3
  814.0 139.5 %copy-start.13 = (f32[3]{0:T(128)S(1)}, f32[3]{0:T(128)}, u32[]{:S(2)}) copy-start(f32[3]{0:T(128)} %constant.120.clone) | copy-start | bytes 40
Sparse Core Ops, SparseCore 0:
  488.9 46.8 all-gather.1
Sparse Core Ops, SparseCore 1:
  823.6 129.8 all-reduce.1
where the time goes:
time: 1130 us
  local copies, waits for them, and re-layouts  359 us (32%)
  other arithmetic  212 us (19%)
  matrix products  193 us (17%)
  loops' own time  163 us (14%)
  waiting for transfers between devices  106 us (9%)
  blocking collectives  41.4 us (4%)
  starting transfers between devices  37.4 us (3%)
  between operations  16.7 us (1%)
    dot_general x48, matrix products, one_row(): jnp.einsum('ckij,ckj->ci', weight, near_val, precision=lax.Precision.HIGH...  193 us
    another operation x3, loops' own time, pair_sums(): return lax.map(one_row, jnp.arange(row_count, dtype=jnp.int32))  163 us
    scatter-add x1, other arithmetic, shards(): jax.ops.segment_sum(stacked, wall_body.reshape(-1), num_segments=BODIES)  94 us
    reduce_sum x48, other arithmetic, one_row(): weight_sum = jnp.sum(weight, axis=(1, 3))  90.2 us
    psum x1, waiting for transfers between devices, shards(): totals, density_error = lax.psum((partials, error_local), ('tile', 'body'))  86.6 us
    gather x1, local copies, waits for them, and re-layouts, shards(): jnp.take(full_state[0:3], index_flat, axis=1).reshape(wall_arm.shape)  59.9 us
    gather x1, local copies, waits for them, and re-layouts, shards(): jnp.take(full_state[3:6], index_flat, axis=1).reshape(wall_arm.shape)  59.8 us
    gather x144, local copies, waits for them, and re-layouts, one_row(): jnp.take_along_axis(jnp.transpose(shifted_pos, (2, 0, 1, 3)), code_list[:...  53 us
  transfers between devices with their start and end apart: 18, of which 7 were waited for; matrix products, arithmetic and copies ran while one was open for 24% of the time, Pallas kernels for 0%

commit v1 on v0

--- a/solution.py
+++ b/solution.py
@@ -2,6 +2,7 @@
 import jax.numpy as jnp
 from jax import lax
 from jax.sharding import PartitionSpec as P
+from jax.lax import psum
 
 SWEEPS = 2
 BODIES = 30720
@@ -120,7 +121,7 @@
     own_params = jnp.concatenate(
         [linear_velocity, angular_velocity, inverse_mass[None], inverse_inertia], 0
     )
-    totals, density_error = lax.psum((partials, error_local), ("tile", "body"))
+    totals, density_error = psum(psum((partials, error_local), "tile"), "body")
     all_params = lax.all_gather(own_params, "body", axis=1, tiled=True)
     full_state = advance(all_params, totals)
     own_state = lax.dynamic_slice_in_dim(full_state, first_owned, owned, 1)

time: 1130 us -> 1110 us (0.982)
  blocking collectives: 41.4 us -> 25.6 us
    psum x1 -> x2, blocking collectives: 41.4 us -> 25.6 us  [shards(): totals, density_error = psum(psum((partials, error_local), 'tile'), 'body')]
    psum x1 -> x2, waiting for transfers between devices: 86.6 us -> 77.8 us  [shards(): totals, density_error = psum(psum((partials, error_local), 'tile'), 'body')]
  transfers between devices with their start and end apart: 18 -> 19, of which waited for: 7 -> 8; matrix products, arithmetic and copies ran while one was open for 24% -> 1% of each run, Pallas kernels for 0% -> 0%
where the time goes in v1:
time: 1110 us
  local copies, waits for them, and re-layouts  360 us (32%)
  other arithmetic  212 us (19%)
  matrix products  193 us (17%)
  loops' own time  163 us (15%)
  waiting for transfers between devices  98.4 us (9%)
  starting transfers between devices  37.5 us (3%)
  blocking collectives  25.6 us (2%)
  between operations  16.7 us (2%)
    dot_general x48, matrix products, one_row(): jnp.einsum('ckij,ckj->ci', weight, near_val, precision=lax.Precision.HIGH...  193 us
    another operation x3, loops' own time, pair_sums(): return lax.map(one_row, jnp.arange(row_count, dtype=jnp.int32))  163 us
    scatter-add x1, other arithmetic, shards(): jax.ops.segment_sum(stacked, wall_body.reshape(-1), num_segments=BODIES)  94.1 us
    reduce_sum x48, other arithmetic, one_row(): weight_sum = jnp.sum(weight, axis=(1, 3))  90.2 us
    psum x2, waiting for transfers between devices, shards(): totals, density_error = psum(psum((partials, error_local), 'tile'), 'body')  77.8 us
    gather x1, local copies, waits for them, and re-layouts, shards(): jnp.take(full_state[0:3], index_flat, axis=1).reshape(wall_arm.shape)  60.2 us
    gather x1, local copies, waits for them, and re-layouts, shards(): jnp.take(full_state[3:6], index_flat, axis=1).reshape(wall_arm.shape)  60.2 us
    gather x144, local copies, waits for them, and re-layouts, one_row(): jnp.take_along_axis(jnp.transpose(shifted_pos, (2, 0, 1, 3)), code_list[:...  53 us
  transfers between devices with their start and end apart: 19, of which 8 were waited for; matrix products, arithmetic and copies ran while one was open for 1% of the time, Pallas kernels for 0%

profile of v1, /device:TPU:0, one launch (start us, length us, event | category | flops | bytes accessed | tf_op | source)
XLA Modules:
  0.0 1105.3 jit_solution(7589567651568128614)
XLA Ops:
  13.8 4.5 collective-permute-start
  27.3 4.5 collective-permute-start.2
  33.4 4.2 collective-permute-done.3
  37.8 214.1 %while.36 = (s32[]{:T(128)}, f32[16,8,128]{2,1,0:T(8,128)S(1)}, f32[16,8,128]{2,1,0:T(8,128)S(1)}, s32[16]{0:T(128)S(1)}, f32[3,16,8,128]{3,2,1,0:T(8,128)}, /*i...) while((s32[]{:T(128)}, f32[16,8,128]{2,1,0:T(8,128)S(1)}, ...), condition=%wide.region_2.0_spmd, body=%wide.region_0.4_spmd.sunk | while | flops 27549932 | bytes 1204188 | solution.py:62
  47.2 4.0 fusion.81
  60.6 4.0 fusion.81
  74.0 4.0 fusion.81
  87.4 4.0 fusion.81
  100.7 4.0 fusion.81
  114.1 4.0 fusion.81
  127.5 4.0 fusion.81
  140.9 4.0 fusion.81
  154.3 4.0 fusion.81
  167.7 4.0 fusion.81
  181.0 4.0 fusion.81
  194.4 4.0 fusion.81
  207.8 4.0 fusion.81
  221.2 4.0 fusion.81
  234.6 4.0 fusion.81
  248.0 4.0 fusion.81
  254.7 5.0 collective-permute-done.9
  264.6 4.1 collective-permute-done.11
  268.8 214.1 %while.37 = (s32[]{:T(128)}, f32[16,8,128]{2,1,0:T(8,128)S(1)}, f32[16,8,128]{2,1,0:T(8,128)S(1)}, s32[16]{0:T(128)S(1)}, f32[3,16,8,128]{3,2,1,0:T(8,128)}, /*i...) while((s32[]{:T(128)}, f32[16,8,128]{2,1,0:T(8,128)S(1)}, ...), condition=%wide.region_5.8_spmd, body=%wide.region_3.7_spmd.sunk | while | flops 27549932 | bytes 1204188 | solution.py:62
  278.2 4.0 fusion.85
  291.5 4.0 fusion.85
  304.9 4.0 fusion.85
  318.3 4.0 fusion.85
  331.7 4.0 fusion.85
  345.1 4.0 fusion.85
  358.4 4.0 fusion.85
  371.8 4.0 fusion.85
  385.2 4.0 fusion.85
  398.6 4.0 fusion.85
  412.0 4.0 fusion.85
  425.4 4.0 fusion.85
  438.7 4.0 fusion.85
  452.1 4.0 fusion.85
  465.5 4.0 fusion.85
  478.9 4.0 fusion.85
  499.9 214.1 %while.38 = (s32[]{:T(128)}, f32[16,8,128]{2,1,0:T(8,128)S(1)}, f32[16,8,128]{2,1,0:T(8,128)S(1)}, s32[16]{0:T(128)S(1)}, f32[3,16,8,128]{3,2,1,0:T(8,128)}, /*i...) while((s32[]{:T(128)}, f32[16,8,128]{2,1,0:T(8,128)S(1)}, ...), condition=%wide.region_8.11_spmd, body=%wide.region_6.10_spmd.sunk | while | flops 27549932 | bytes 1204188 | solution.py:62
  509.2 4.0 fusion.89
  522.6 4.0 fusion.89
  536.0 4.0 fusion.89
  549.4 4.0 fusion.89
  562.7 4.0 fusion.89
  576.1 4.0 fusion.89
  589.5 4.0 fusion.89
  602.9 4.0 fusion.89
  643.0 4.0 fusion.89
  696.5 4.0 fusion.89
  714.5 5.3 copy.268
  719.8 94.1 %scatter_custom_fusion = f32[30720,6]{1,0:T(8,128)} fusion(s32[16384]{0:T(1024)S(1)} %bitcast.478, f32[16384,6]{1,0:T(8,128)} %copy.268, f32[]{:T(128)} %constant.113.clone.1), kind=kCustom, calls=%fused_computation.226 | custom fusion | flops 98304 | bytes 737792 | tf_op jit(solution)/shard_map/scatter-add | solution.py:118
  813.9 9.6 copy.269
  824.6 56.1 %all-reduce.3.cloned.1.call-done = f32[6,30720]{1,0:T(8,128)} async-done(((f32[6,30720]{1,0:T(8,128)}), f32[6,30720]{1,0:T(8,128)}) %all-reduce.3.cloned.1.call-update) | async-done | bytes 737296 | tf_op jit(solution)/shard_map/psum | solution.py:124
  881.5 12.7 %psum.30 = f32[]{:T(128)} all-reduce(f32[]{:T(128)S(6)} %div.15), channel_id=1, replica_groups=mesh['tile'=8,'body'=4] {'tile'}, use_global_device_ids=true, to_apply=%region_13.17 | all-reduce | flops 1 | bytes 8 | tf_op jit(solution)/shard_map/psum | solution.py:124
  894.2 12.9 %psum.31 = f32[]{:T(128)} all-reduce(f32[]{:T(128)} %psum.30), channel_id=1, replica_groups=mesh['tile'=8,'body'=4] {'body'}, use_global_device_ids=true, to_apply=%region_14.18 | all-reduce | flops 1 | bytes 8 | tf_op jit(solution)/shard_map/psum | solution.py:124
  908.4 21.7 %all-reduce.5.cloned.1.call-done = f32[6,30720]{1,0:T(8,128)} async-done(((f32[6,30720]{1,0:T(8,128)}), f32[6,30720]{1,0:T(8,128)}) %all-reduce.5.cloned.1.call-update) | async-done | bytes 737296 | tf_op jit(solution)/shard_map/psum | solution.py:124
  933.4 7.8 copy.271
  941.1 7.7 copy.270
  949.7 60.2 %gather_fusion.7 = f32[16384,3]{1,0:T(8,128)} fusion(f32[3,30720]{0,1:T(8,128)} %copy.271, s32[16384]{0:T(1024)S(1)} %fusion.58), kind=kCustom, calls=%fused_computation.7.clone | custom fusion | bytes 458752 | tf_op jit(solution)/shard_map/jit(_take)/gather | solution.py:130
  1009.9 60.2 %gather_fusion.6 = f32[16384,3]{1,0:T(8,128)} fusion(f32[3,30720]{0,1:T(8,128)} %copy.270, s32[16384]{0:T(1024)S(1)} %fusion.58), kind=kCustom, calls=%fused_computation.2.clone | custom fusion | bytes 458752 | tf_op jit(solution)/shard_map/jit(_take)/gather | solution.py:129
  1070.1 10.8 select_bitcast_fusion.3
  1080.8 11.0 slice_reduce_fusion.1
  1091.9 5.2 copy.272
  (1891 shorter events, 359.7 us)
Async XLA Ops:
  8.0 872.7 %all-reduce.3.cloned.1.call-start = ((), (), s32[]{:S(2)}) async-start(), calls=%async_computation.1 | async-start | bytes 1966080 | tf_op jit(solution)/shard_map/psum | solution.py:124
  8.8 12.5 %collective-permute-start.5 = (f32[1,8,128]{2,1,0:T(8,128)S(1)}, f32[1,8,128]{2,1,0:T(8,128)S(1)}, u32[]{:S(2)}, u32[]{:S(2)}) collective-permute-start(f32[1,8,128]{2,1,0:T(8,128)S(1)} %get-tuple-element.378), channel_id=1, source_target_pairs={{4,0},{8,4},{12,8},{16,12},{20,16},{24,20},{28,24},{5,1},{9,5},{13... | collective-permute-start | bytes 12296 | tf_op jit(solution)/shard_map/ppermute | solution.py:25
  10.0 10.4 collective-permute-start.4
  13.8 12.3 %collective-permute-start = (f32[3,1,8,128]{3,0,2,1:T(4,128)S(1)}, f32[3,1,8,128]{3,0,2,1:T(4,128)S(1)}, u32[]{:S(2)}, u32[]{:S(2)}) collective-permute-start(f32[3,1,8,128]{3,0,2,1:T(4,128)S(1)} %copy.294), channel_id=1, source_target_pairs={{0,4},{4,8},{8,12},{12,16},{16,20},{20,24},{24,28},{1,5},{5,9},{9,... | collective-permute-start | bytes 36872 | tf_op jit(solution)/shard_map/ppermute | solution.py:22
  18.3 8.9 collective-permute-start.1
  21.3 11.8 %collective-permute-start.6 = (f32[18,1,128]{2,1,0:T(1,128)S(1)}, f32[18,1,128]{2,1,0:T(1,128)S(1)}, u32[]{:S(2)}, u32[]{:S(2)}) collective-permute-start(f32[18,1,128]{2,1,0:T(1,128)S(1)} %get-tuple-element.372), channel_id=1, source_target_pairs={{0,1},{1,2},{2,3},{4,5},{5,6},{6,7},{8,9},{9,10},{10,11},{12,13},{... | collective-permute-start | bytes 27656 | tf_op jit(solution)/shard_map/ppermute | solution.py:22
  24.8 8.3 collective-permute-start.7
  27.3 6.2 collective-permute-start.2
  31.8 5.9 collective-permute-start.3
  37.8 214.2 %copy-start.4 = (f32[16,8,128]{2,1,0:T(8,128)S(1)}, f32[16,8,128]{2,1,0:T(8,128)}, u32[]{:S(2)}) copy-start(f32[16,8,128]{2,1,0:T(8,128)} %param.28) | copy-start | bytes 196612
  37.8 214.2 %copy-start.6 = (f32[16,8,128]{2,1,0:T(8,128)S(1)}, f32[16,8,128]{2,1,0:T(8,128)}, u32[]{:S(2)}) copy-start(f32[16,8,128]{2,1,0:T(8,128)} %param.29) | copy-start | bytes 196612
  37.8 214.2 %copy-start.7 = (f32[16,8,128]{2,1,0:T(8,128)S(1)}, f32[16,8,128]{2,1,0:T(8,128)}, u32[]{:S(2)}) copy-start(f32[16,8,128]{2,1,0:T(8,128)} %param.30) | copy-start | bytes 196612
  252.1 2.6 collective-permute-start.8
  253.4 6.3 collective-permute-start.9
  259.7 5.0 collective-permute-start.10
  263.2 5.6 collective-permute-start.11
  268.8 226.9 %copy-start.12 = (f32[7680]{0:T(1024)S(1)}, f32[7680]{0:T(1024)}, u32[]{:S(2)}) copy-start(f32[7680]{0:T(1024)} %param.39) | copy-start | bytes 92164
  483.6 16.3 %copy-start.2 = (f32[16,8,128]{2,1,0:T(8,128)}, f32[16,8,128]{2,1,0:T(8,128)S(1)}, u32[]{:S(2)}) copy-start(f32[16,8,128]{2,1,0:T(8,128)S(1)} %get-tuple-element.360) | copy-start | bytes 196612
  483.6 4.1 collective-permute-start.12
  486.4 4.3 collective-permute-start.13
  490.7 5.1 collective-permute-start.14
  494.2 5.6 collective-permute-start.15
  499.8 214.1 %copy-start.11 = (s32[16,8,128]{2,1,0:T(8,128)S(1)}, s32[16,8,128]{2,1,0:T(8,128)}, u32[]{:S(2)}) copy-start(s32[16,8,128]{2,1,0:T(8,128)} %param.35) | copy-start | bytes 196612
  499.8 214.2 %copy-start = (f32[3,16,8,128]{3,2,1,0:T(8,128)S(1)}, f32[3,16,8,128]{3,2,1,0:T(8,128)}, u32[]{:S(2)}) copy-start(f32[3,16,8,128]{3,2,1,0:T(8,128)} %param.33) | copy-start | bytes 589828
  499.8 214.4 %copy-start.1 = (f32[3,16,8,128]{3,2,1,0:T(8,128)S(1)}, f32[3,16,8,128]{3,2,1,0:T(8,128)}, u32[]{:S(2)}) copy-start(f32[3,16,8,128]{3,2,1,0:T(8,128)} %param.34) | copy-start | bytes 589828
  714.0 5.8 copy-start.3
  714.5 5.3 copy-start.5
  813.9 9.7 copy-start.8
  813.9 9.7 copy-start.9
  813.9 9.7 copy-start.10
  823.4 106.6 %copy-start.13 = (f32[3]{0:T(128)S(1)}, f32[3]{0:T(128)}, u32[]{:S(2)}) copy-start(f32[3]{0:T(128)} %constant.120.clone) | copy-start | bytes 40
  823.5 83.6 %all-gather.2.cloned.1.call-start = ((), (), s32[]{:S(2)}) async-start(), calls=%async_computation | async-start | bytes 2457600 | tf_op jit(solution)/shard_map/all_gather | solution.py:125
  824.5 105.5 %all-reduce.5.cloned.1.call-start = ((), (), s32[]{:S(2)}) async-start(), calls=%async_computation.2 | async-start | bytes 1966080 | tf_op jit(solution)/shard_map/psum | solution.py:124
Sparse Core Ops, SparseCore 0:
  823.6 57.1 all-reduce.2
Sparse Core Ops, SparseCore 1:
  825.5 44.0 all-gather.1
  880.8 49.2 all-reduce.4
